TPU v7x, 256 devices: a whole 4x4x8 slice. The times are simulated.
256 devices in a mesh: row: 64 (over y, z, core), col: 4 (over x).
Axes of the slice: x: 4, y: 4, z: 8, core: 2. Of those that a mesh axis runs over, the one named last changes fastest.
Arguments:
- factor: float32 [8192, 8192], P('row', 'col'), may hold values from -0.125 to 0.125
- rhs: float32 [8192, 512], P('row', 'col'), may hold values from -6 to 6
- parent: int32 [7], replicated, may hold values from 4 to 6, as said below
- bounds: int32 [8], replicated, may hold values from 0 to 64, as said below
- slot: int32 [64], replicated, may hold values from 0 to 63, each once
- structure: int32 [7, 64], replicated, may hold values 0 or 1
Outputs:
- solution: float32 [8192, 512], P('row', 'col')
Inputs may be any that keep to these rules, and one draw needn't show every extreme that they name: parent[s] is 4 or 5 for s = 0 to 3, and 6 for s = 4, 5, 6 (the root is its own entry). bounds[0] = 0, bounds[7] = 64, strictly increasing; supernode s holds logical blocks bounds[s] to bounds[s+1] - 1. `slot`: a permutation.
All inputs are finite; a program needn't handle non-finite values.
Results may differ from a plain program's by a relative error of at most 0.0001.
Values sent between devices are 32-bit elements; how exact they have to be, the bound alone decides.
A program may use at most 64 MiB of HBM per device.

v0:
```python
import jax
import jax.numpy as jnp
from jax import lax
from jax.sharding import PartitionSpec as P

B = 128
RB = 1


def block_masks(parent, bounds, slot, structure):
    count = slot.shape[0]
    ar = jnp.arange(count, dtype=jnp.int32)
    logical = jnp.sum(jnp.where(slot[:, None] == ar[None, :], ar[:, None], 0), axis=0)
    node = jnp.sum((logical[:, None] >= bounds[None, 1:7]).astype(jnp.int32), axis=1)
    level = (node >= 4).astype(jnp.int32) + (node >= 6).astype(jnp.int32)
    nodes = jnp.arange(7, dtype=jnp.int32)
    grand = parent[parent]
    ancestor = ((nodes[None, :] == parent[:, None]) | (nodes[None, :] == grand[:, None])) & (
        nodes[None, :] != nodes[:, None]
    )
    node_hot = (node[:, None] == nodes[None, :]).astype(jnp.float32)
    perm_hot = (logical[:, None] == ar[None, :]).astype(jnp.float32)
    listed_store = jnp.dot(
        structure.astype(jnp.float32), perm_hot.T, precision=lax.Precision.HIGHEST
    )
    anc_pairs = jnp.dot(
        node_hot,
        jnp.dot(ancestor.astype(jnp.float32), node_hot.T, precision=lax.Precision.HIGHEST),
        precision=lax.Precision.HIGHEST,
    )
    list_pairs = jnp.dot(node_hot, listed_store, precision=lax.Precision.HIGHEST)
    link = (anc_pairs * list_pairs).T > 0.5
    same = node[:, None] == node[None, :]
    return (level, same, link)


def masked(block_rows, mask):
    rblocks, width = mask.shape
    bsz = block_rows.shape[0] // rblocks
    shaped = block_rows.reshape(rblocks, bsz, width, bsz) * mask[:, None, :, None].astype(
        jnp.float32
    )
    return shaped.reshape(block_rows.shape)


def body(factor, rhs, parent, bounds, slot, structure):
    level, same, link = block_masks(parent, bounds, slot, structure)
    first = lax.axis_index("row") * RB
    level_mine = lax.dynamic_slice_in_dim(level, first, RB, 0)
    same_mine = lax.dynamic_slice_in_dim(same, first, RB, 0)
    link_mine = lax.dynamic_slice_in_dim(link, first, RB, 0)
    full_rows = lax.all_gather(factor, "col", axis=1, tiled=True)
    diag_part = masked(full_rows, same_mine)
    link_part = masked(full_rows, link_mine)

    def product(matrix, vector):
        return jnp.dot(
            matrix,
            lax.all_gather(vector, "row", axis=0, tiled=True),
            precision=lax.Precision.HIGHEST,
            preferred_element_type=jnp.float32,
        )

    pieces = [rhs]
    accums = [jnp.zeros(p.shape, jnp.float32) for p in pieces]
    results = [jnp.zeros(p.shape, jnp.float32) for p in pieces]
    for section in range(3):
        rows = jnp.repeat(level_mine == section, B)[:, None]
        solved = jnp.where(rows, product(diag_part, pieces[0] - accums[0]), 0.0)
        results[0] = results[0] + solved
        if section < 2:
            accums[0] = accums[0] + product(link_part, solved)
    return results[0]


def solution(mesh):
    in_specs = (P("row", "col"), P("row", "col"), P(), P(), P(), P())
    out_specs = P("row", "col")
    return jax.shard_map(body, mesh=mesh, in_specs=in_specs, out_specs=out_specs, check_vma=False)
```

profile of v0, /device:TPU:1, one launch (start us, length us, event | category | flops | bytes accessed | tf_op | source)
XLA Modules:
  0.0 501.4 jit_solution(158808282834339269)
XLA Ops:
  6.5 0.0 all-gather.7.cloned.1.call-start
  6.5 0.7 all-gather.7.cloned.1.call-update
  7.3 0.0 all-gather.9.cloned.1.call-start
  7.3 0.7 all-gather.9.cloned.1.call-update
  8.0 0.0 all-gather.11.cloned.1.call-start
  8.1 0.7 slice.3
  8.8 0.7 select_reduce_fusion
  9.5 0.1 convert_reduce_fusion
  9.6 0.6 dynamic-slice
  10.2 0.7 dynamic_slice.9
  11.6 0.7 fusion.48
  12.2 0.1 broadcast_bitcast_fusion.1
  12.3 51.4 %all-gather.7.cloned.1.call-done = f32[128,8192]{1,0:T(8,128)} async-done(((f32[128,2048]{1,0:T(8,128)}), f32[128,8192]{1,0:T(8,128)}) %all-gather.7.cloned.1.call-update) | async-done | bytes 4194320 | tf_op jit(solution)/shard_map/all_gather | solution.py:52
  63.8 82.7 %all-gather.9.cloned.1.call-done = f32[8192,128]{1,0:T(8,128)} async-done(((f32[128,128]{1,0:T(8,128)}), f32[8192,128]{1,0:T(8,128)}) %all-gather.9.cloned.1.call-update) | async-done | bytes 4194320 | tf_op jit(solution)/shard_map/all_gather | solution.py:59
  146.5 0.0 copy-start
  146.5 0.0 copy-start.4
  146.5 0.0 copy-start.1
  146.5 8.4 %fusion.15 = f32[128,128]{1,0:T(8,128)} fusion(f32[8192,128]{1,0:T(8,128)} %all-gather.9.cloned.1.call-done, f32[128,8192]{1,0:T(8,128)} %all-gather.7.cloned.1.call-done, f32[8192]{0:T(1024)S(1)} %broadcast_bitcast_fusion.1, pred[]{:T(512)} %bitcast), kind=kOutput, calls=%fused_computation.16 | convolution fusion | flops 1611677696 | bytes 8486913 | tf_op jit(solution)/shard_map/dot_general | solution.py:57
  154.9 0.0 all-gather.11.cloned.1.call-update
  154.9 0.0 all-gather.13.cloned.1.call-start
  155.0 0.0 copy-done
  155.0 0.6 gather_fusion
  155.6 0.2 fusion.35
  155.8 0.0 copy-done.4
  155.8 0.2 fusion.36
  156.0 0.3 fusion.33
  156.3 0.2 fusion.34
  156.6 0.1 broadcast_bitcast_fusion
  156.7 74.7 %all-gather.11.cloned.1.call-done = f32[8192,128]{1,0:T(8,128)} async-done(((f32[128,128]{1,0:T(8,128)}), f32[8192,128]{1,0:T(8,128)}) %all-gather.11.cloned.1.call-update) | async-done | bytes 4194320 | tf_op jit(solution)/shard_map/all_gather | solution.py:59
  231.4 0.0 copy-done.1
  231.4 8.4 %fusion.50 = (f32[128,128]{1,0:T(8,128)}, f32[128,128]{1,0:T(8,128)S(1)}) fusion(f32[128,128]{1,0:T(8,128)S(1)} %copy-done.1, f32[8192,128]{1,0:T(8,128)} %all-gather.11.cloned.1.call-done, f32[128,8192]{1,0:T(8,128)} %all-gather.7.cloned.1.call-done, f32[8192]{0:T(1024)S(1)} %broadcast_bitcast_fusion), kind=kOutput, calls=%fused_computation.55 | convolution fusion | flops 1611677696 | bytes 8617984 | tf_op jit(solution)/shard_map/dot_general | solution.py:57
  239.8 0.0 all-gather.13.cloned.1.call-update
  239.8 0.2 all-gather.15.cloned.1.call-start
  240.7 75.6 %all-gather.13.cloned.1.call-done = f32[8192,128]{1,0:T(8,128)} async-done(((f32[128,128]{1,0:T(8,128)}), f32[8192,128]{1,0:T(8,128)}) %all-gather.13.cloned.1.call-update) | async-done | bytes 4194320 | tf_op jit(solution)/shard_map/all_gather | solution.py:59
  316.3 8.4 %fusion.18 = f32[128,128]{1,0:T(8,128)} fusion(f32[8192,128]{1,0:T(8,128)} %all-gather.13.cloned.1.call-done, f32[128,8192]{1,0:T(8,128)} %all-gather.7.cloned.1.call-done, f32[8192]{0:T(1024)S(1)} %broadcast_bitcast_fusion.1, pred[]{:T(512)} %bitcast.3), kind=kOutput, calls=%fused_computation.17 | convolution fusion | flops 1611677696 | bytes 8486913 | tf_op jit(solution)/shard_map/dot_general | solution.py:57
  324.7 0.0 all-gather.15.cloned.1.call-update
  324.7 0.0 all-gather.17.cloned.1.call-start
  324.8 76.4 %all-gather.15.cloned.1.call-done = f32[8192,128]{1,0:T(8,128)} async-done(((f32[128,128]{1,0:T(8,128)}), f32[8192,128]{1,0:T(8,128)}) %all-gather.15.cloned.1.call-update) | async-done | bytes 4194320 | tf_op jit(solution)/shard_map/all_gather | solution.py:59
  401.2 0.0 copy-start.2
  401.2 0.0 copy-start.3
  401.2 8.4 %fusion.30 = f32[128,128]{1,0:T(8,128)} fusion(f32[128,128]{1,0:T(8,128)S(1)} %copy-done.1, f32[128,128]{1,0:T(8,128)S(1)} %get-tuple-element.6, f32[8192,128]{1,0:T(8,128)} %all-gather.15.cloned.1.call-done, f32[128,8192]{1,0:T(8,128)} %all-gather.7.cloned.1.call-done, f32[8192]{0:T(1024)S(1)} %broadcast_bitcast_fusion), kind=kOutput, calls=%fused_computation.21 | convolution fusion | flops 1611694080 | bytes 8617984 | tf_op jit(solution)/shard_map/dot_general | solution.py:57
  409.6 0.0 all-gather.17.cloned.1.call-update
  410.3 75.8 %all-gather.17.cloned.1.call-done = f32[8192,128]{1,0:T(8,128)} async-done(((f32[128,128]{1,0:T(8,128)}), f32[8192,128]{1,0:T(8,128)}) %all-gather.17.cloned.1.call-update) | async-done | bytes 4194320 | tf_op jit(solution)/shard_map/all_gather | solution.py:59
  486.1 0.0 copy-done.2
  486.1 0.0 copy-done.3
  486.1 8.4 %fusion.24 = f32[128,128]{1,0:T(8,128)} fusion(f32[8192,128]{1,0:T(8,128)} %all-gather.17.cloned.1.call-done, f32[128,8192]{1,0:T(8,128)} %all-gather.7.cloned.1.call-done, f32[8192]{0:T(1024)S(1)} %broadcast_bitcast_fusion.1, f32[128,128]{1,0:T(8,128)S(1)} %copy-done.2, f32[128,128]{1,0:T(8,128)S(1)} %copy-done.3, pred[]{:T(512)} %bitcast.6), kind=kOutput, calls=%fused_computation.19 | convolution fusion | flops 1611710464 | bytes 8617985 | tf_op jit(solution)/shard_map/dot_general | solution.py:57
  (4 shorter events, 0.0 us)
Async XLA Ops:
  6.5 57.2 %all-gather.7.cloned.1.call-start = ((), (), s32[]{:S(2)}) async-start(), calls=%async_computation | async-start | bytes 5242880 | tf_op jit(solution)/shard_map/all_gather | solution.py:52
  7.3 139.2 %all-gather.9.cloned.1.call-start = ((), (), s32[]{:S(2)}) async-start(), calls=%async_computation.1 | async-start | bytes 4259840 | tf_op jit(solution)/shard_map/all_gather | solution.py:59
  8.0 223.4 %all-gather.11.cloned.1.call-start = ((), (), s32[]{:S(2)}) async-start(), calls=%async_computation.2 | async-start | bytes 4259840 | tf_op jit(solution)/shard_map/all_gather | solution.py:59
  146.5 8.5 %copy-start = (s32[7]{0:T(128)S(1)}, s32[7]{0:T(128)}, u32[]{:S(2)}) copy-start(s32[7]{0:T(128)} %param.8) | copy-start | bytes 88
  146.5 9.4 %copy-start.4 = (s32[7,64]{1,0:T(8,128)S(1)}, s32[7,64]{1,0:T(8,128)}, u32[]{:S(2)}) copy-start(s32[7,64]{1,0:T(8,128)} %param.11) | copy-start | bytes 5380
  146.5 84.9 %copy-start.1 = (f32[128,128]{1,0:T(8,128)S(1)}, f32[128,128]{1,0:T(8,128)}, u32[]{:S(2)}) copy-start(f32[128,128]{1,0:T(8,128)} %param.7) | copy-start | bytes 196612
  154.9 161.4 %all-gather.13.cloned.1.call-start = ((), (), s32[]{:S(2)}) async-start(), calls=%async_computation.3 | async-start | bytes 4259840 | tf_op jit(solution)/shard_map/all_gather | solution.py:59
  239.8 161.4 %all-gather.15.cloned.1.call-start = ((), (), s32[]{:S(2)}) async-start(), calls=%async_computation.4 | async-start | bytes 4259840 | tf_op jit(solution)/shard_map/all_gather | solution.py:59
  324.7 161.4 %all-gather.17.cloned.1.call-start = ((), (), s32[]{:S(2)}) async-start(), calls=%async_computation.5 | async-start | bytes 4259840 | tf_op jit(solution)/shard_map/all_gather | solution.py:59
  401.2 84.9 %copy-start.2 = (f32[128,128]{1,0:T(8,128)S(1)}, f32[128,128]{1,0:T(8,128)}, u32[]{:S(2)}) copy-start(f32[128,128]{1,0:T(8,128)} %fusion.15) | copy-start | bytes 196612
  401.2 84.9 %copy-start.3 = (f32[128,128]{1,0:T(8,128)S(1)}, f32[128,128]{1,0:T(8,128)}, u32[]{:S(2)}) copy-start(f32[128,128]{1,0:T(8,128)} %fusion.18) | copy-start | bytes 196612
Sparse Core Ops, SparseCore 0:
  9.2 54.5 all-gather.6
  66.5 79.8 all-gather.8
  155.0 76.3 all-gather.10
  239.9 76.3 all-gather.12
  324.8 76.3 all-gather.14
  409.8 76.3 all-gather.16
where the time goes:
time: 501 us
  waiting for transfers between devices  438 us (87%)
  matrix products  42.9 us (9%)
  between operations  15.6 us (3%)
    all_gather x5, waiting for transfers between devices, product(): lax.all_gather(vector, 'row', axis=0, tiled=True)  385 us
    all_gather x1, waiting for transfers between devices, body(): full_rows = lax.all_gather(factor, 'col', axis=1, tiled=True)  51.4 us
    dot_general x5, matrix products, product(): jnp.dot(matrix, lax.all_gather(vector, 'row', axis=0, tiled=True), precis...  42 us
  transfers between devices with their start and end apart: 6, of which 6 were waited for; matrix products, arithmetic and copies ran while one was open for 1% of the time, Pallas kernels for 0%

commit v1 on v0

--- a/solution.py
+++ b/solution.py
@@ -5,6 +5,16 @@
 
 B = 128
 RB = 1
+
+
+def lead_scales_for(axis_name, page):
+    w1 = jax.lax.all_to_all(
+        jnp.stack([page for _ in range(jax.lax.axis_size(axis_name))]),
+        axis_name=axis_name,
+        split_axis=0,
+        concat_axis=0,
+    )
+    return jnp.concatenate(w1, axis=0)
 
 
 def block_masks(parent, bounds, slot, structure):
@@ -56,7 +66,7 @@
     def product(matrix, vector):
         return jnp.dot(
             matrix,
-            lax.all_gather(vector, "row", axis=0, tiled=True),
+            lead_scales_for("row", vector),
             precision=lax.Precision.HIGHEST,
             preferred_element_type=jnp.float32,
         )

time: 501 us -> 578 us (1.15)
  blocking collectives: 0 us -> 102 us
  waiting for transfers between devices: 438 us -> 378 us
  starting transfers between devices: 0.38 us -> 31.5 us
  local copies, waits for them, and re-layouts: 2.79 us -> 13.3 us
  matrix products: 42.9 us -> 37 us
    all_gather x5 -> x0, waiting for transfers between devices: 385 us -> none  [product(): lax.all_gather(vector, 'row', axis=0, tiled=True)]
    all_to_all x0 -> x4, waiting for transfers between devices: none -> 326 us  [lead_scales_for(): jax.lax.all_to_all(jnp.stack([page for _ in range(jax.lax.axis_size(axis_...]
    all_to_all x0 -> x1, blocking collectives: none -> 102 us  [lead_scales_for(): jax.lax.all_to_all(jnp.stack([page for _ in range(jax.lax.axis_size(axis_...]
    all_to_all x0 -> x4, starting transfers between devices: none -> 31.5 us  [lead_scales_for(): jax.lax.all_to_all(jnp.stack([page for _ in range(jax.lax.axis_size(axis_...]
    another operation x0 -> x5, local copies, waits for them, and re-layouts: none -> 11.2 us  [lead_scales_for(): jnp.stack([page for _ in range(jax.lax.axis_size(axis_name))])]
    dot_general x5, matrix products: 42 us -> 36.1 us  [product(): jnp.dot(matrix, lead_scales_for('row', vector), precision=lax.Precision.H...]
  transfers between devices with their start and end apart: 6 -> 5, of which waited for: 6 -> 5; matrix products, arithmetic and copies ran while one was open for 1% -> 1% of each run, Pallas kernels for 0% -> 0%
where the time goes in v1:
time: 578 us
  waiting for transfers between devices  378 us (65%)
  blocking collectives  102 us (18%)
  matrix products  37 us (6%)
  starting transfers between devices  31.5 us (5%)
  between operations  15.4 us (3%)
  local copies, waits for them, and re-layouts  13.3 us (2%)
    all_to_all x4, waiting for transfers between devices, lead_scales_for(): jax.lax.all_to_all(jnp.stack([page for _ in range(jax.lax.axis_size(axis_...  326 us
    all_to_all x1, blocking collectives, lead_scales_for(): jax.lax.all_to_all(jnp.stack([page for _ in range(jax.lax.axis_size(axis_...  102 us
    all_gather x1, waiting for transfers between devices, body(): full_rows = lax.all_gather(factor, 'col', axis=1, tiled=True)  50.8 us
    dot_general x5, matrix products, product(): jnp.dot(matrix, lead_scales_for('row', vector), precision=lax.Precision.H...  36.1 us
    all_to_all x4, starting transfers between devices, lead_scales_for(): jax.lax.all_to_all(jnp.stack([page for _ in range(jax.lax.axis_size(axis_...  31.5 us
  transfers between devices with their start and end apart: 5, of which 5 were waited for; matrix products, arithmetic and copies ran while one was open for 1% of the time, Pallas kernels for 0%

profile of v1, /device:TPU:1, one launch (start us, length us, event | category | flops | bytes accessed | tf_op | source)
XLA Modules:
  0.0 577.8 jit_solution(10657999921167004660)
XLA Ops:
  6.5 3.3 stack.10
  9.8 0.0 copy-start.4
  9.8 0.0 copy-start.5
  9.8 13.5 %all-to-all-start = ((f32[64,128,128]{2,1,0:T(8,128)}), f32[64,128,128]{2,1,0:T(8,128)}, u32[]{:S(2)}, u32[]{:S(2)}) async-start(f32[64,128,128]{2,1,0:T(8,128)} %stack.10), calls=%async_computation | async-start | bytes 8388608 | tf_op jit(solution)/shard_map/all_to_all | solution.py:11
  23.3 0.0 all-gather.2.cloned.1.call-start
  23.4 0.7 all-gather.2.cloned.1.call-update
  24.1 0.0 copy-done.4
  24.1 0.1 slice.3
  24.1 0.0 copy-done.5
  24.2 0.1 select_reduce_fusion
  24.2 0.1 convert_reduce_fusion
  24.3 0.6 dynamic-slice
  24.9 0.6 dynamic_slice.9
  26.2 0.7 fusion.48
  26.8 0.1 broadcast_bitcast_fusion.1
  26.9 50.8 %all-gather.2.cloned.1.call-done = f32[128,8192]{1,0:T(8,128)} async-done(((f32[128,2048]{1,0:T(8,128)}), f32[128,8192]{1,0:T(8,128)}) %all-gather.2.cloned.1.call-update) | async-done | bytes 4194320 | tf_op jit(solution)/shard_map/all_gather | solution.py:62
  77.7 41.5 %all-to-all-done = f32[64,128,128]{2,1,0:T(8,128)} async-done(((f32[64,128,128]{2,1,0:T(8,128)}), f32[64,128,128]{2,1,0:T(8,128)}, u32[]{:S(2)}, u32[]{:S(2)}) %all-to-all-start) | async-done | bytes 4194336 | tf_op jit(solution)/shard_map/all_to_all | solution.py:11
  119.2 7.8 %fusion.15 = f32[128,128]{1,0:T(8,128)S(1)} fusion(f32[8192,128]{1,0:T(8,128)} %bitcast.3, f32[128,8192]{1,0:T(8,128)} %all-gather.2.cloned.1.call-done, f32[8192]{0:T(1024)S(1)} %broadcast_bitcast_fusion.1, pred[]{:T(512)} %bitcast), kind=kOutput, calls=%fused_computation.16 | convolution fusion | flops 1611677696 | bytes 8486913 | tf_op jit(solution)/shard_map/dot_general | solution.py:67
  127.0 2.5 stack.11
  129.5 0.0 copy-start
  129.5 0.0 copy-start.3
  129.5 0.0 copy-start.2
  129.5 6.1 %all-to-all-start.1 = ((f32[64,128,128]{2,1,0:T(8,128)}), f32[64,128,128]{2,1,0:T(8,128)}, u32[]{:S(2)}, u32[]{:S(2)}) async-start(f32[64,128,128]{2,1,0:T(8,128)} %stack.11), calls=%async_computation.1 | async-start | bytes 8388608 | tf_op jit(solution)/shard_map/all_to_all | solution.py:11
  135.6 0.0 copy-done
  135.6 0.6 gather_fusion
  136.3 0.2 fusion.35
  136.5 0.0 copy-done.3
  136.5 0.2 fusion.36
  136.7 0.3 fusion.33
  136.9 0.2 fusion.34
  137.2 0.1 broadcast_bitcast_fusion
  137.3 94.2 %all-to-all-done.1 = f32[64,128,128]{2,1,0:T(8,128)} async-done(((f32[64,128,128]{2,1,0:T(8,128)}), f32[64,128,128]{2,1,0:T(8,128)}, u32[]{:S(2)}, u32[]{:S(2)}) %all-to-all-start.1) | async-done | bytes 4194336 | tf_op jit(solution)/shard_map/all_to_all | solution.py:11
  231.5 0.0 copy-done.2
  231.5 7.8 %fusion.50 = (f32[128,128]{1,0:T(8,128)S(1)}, f32[128,128]{1,0:T(8,128)S(1)}) fusion(f32[128,128]{1,0:T(8,128)S(1)} %copy-done.2, f32[8192,128]{1,0:T(8,128)} %bitcast.7, f32[128,8192]{1,0:T(8,128)} %all-gather.2.cloned.1.call-done, f32[8192]{0:T(1024)S(1)} %broadcast_bitcast_fusion), kind=kOutput, calls=%fused_computation.55 | convolution fusion | flops 1611677696 | bytes 8617984 | tf_op jit(solution)/shard_map/dot_general | solution.py:67
  239.3 2.5 stack.12
  241.7 5.9 %all-to-all-start.2 = ((f32[64,128,128]{2,1,0:T(8,128)}), f32[64,128,128]{2,1,0:T(8,128)}, u32[]{:S(2)}, u32[]{:S(2)}) async-start(f32[64,128,128]{2,1,0:T(8,128)} %stack.12), calls=%async_computation.2 | async-start | bytes 8388608 | tf_op jit(solution)/shard_map/all_to_all | solution.py:11
  248.3 95.3 %all-to-all-done.2 = f32[64,128,128]{2,1,0:T(8,128)} async-done(((f32[64,128,128]{2,1,0:T(8,128)}), f32[64,128,128]{2,1,0:T(8,128)}, u32[]{:S(2)}, u32[]{:S(2)}) %all-to-all-start.2) | async-done | bytes 4194336 | tf_op jit(solution)/shard_map/all_to_all | solution.py:11
  343.5 7.8 %fusion.18 = f32[128,128]{1,0:T(8,128)S(1)} fusion(f32[8192,128]{1,0:T(8,128)} %bitcast.8, f32[128,8192]{1,0:T(8,128)} %all-gather.2.cloned.1.call-done, f32[8192]{0:T(1024)S(1)} %broadcast_bitcast_fusion.1, pred[]{:T(512)} %bitcast.4), kind=kOutput, calls=%fused_computation.17 | convolution fusion | flops 1611677696 | bytes 8486913 | tf_op jit(solution)/shard_map/dot_general | solution.py:67
  351.4 0.5 stack.13
  351.9 0.0 copy-start.1
  351.9 102.0 %all_to_all.25 = f32[64,128,128]{2,1,0:T(8,128)S(1)} all-to-all(f32[64,128,128]{2,1,0:T(8,128)S(1)} %stack.13), channel_id=1, replica_groups=mesh['row'=64,'col'=4] {'row'}, dimensions={0} | all-to-all | bytes 8388608 | tf_op jit(solution)/shard_map/all_to_all | solution.py:11
  453.9 0.0 copy-done.1
  453.9 4.3 fusion.30
  458.2 2.5 stack.14
  460.7 6.0 %all-to-all-start.4 = ((f32[64,128,128]{2,1,0:T(8,128)}), f32[64,128,128]{2,1,0:T(8,128)}, u32[]{:S(2)}, u32[]{:S(2)}) async-start(f32[64,128,128]{2,1,0:T(8,128)} %stack.14), calls=%async_computation.4 | async-start | bytes 8388608 | tf_op jit(solution)/shard_map/all_to_all | solution.py:11
  467.3 95.3 %all-to-all-done.4 = f32[64,128,128]{2,1,0:T(8,128)} async-done(((f32[64,128,128]{2,1,0:T(8,128)}), f32[64,128,128]{2,1,0:T(8,128)}, u32[]{:S(2)}, u32[]{:S(2)}) %all-to-all-start.4) | async-done | bytes 4194336 | tf_op jit(solution)/shard_map/all_to_all | solution.py:11
  562.6 8.4 %fusion.24 = f32[128,128]{1,0:T(8,128)} fusion(f32[8192,128]{1,0:T(8,128)} %bitcast.11, f32[128,8192]{1,0:T(8,128)} %all-gather.2.cloned.1.call-done, f32[8192]{0:T(1024)S(1)} %broadcast_bitcast_fusion.1, f32[128,128]{1,0:T(8,128)S(1)} %fusion.15, f32[128,128]{1,0:T(8,128)S(1)} %fusion.18, pred[]{:T(512)} %bitcast.9), kind=kOutput, calls=%fused_computation.19 | convolution fusion | flops 1611710464 | bytes 8617985 | tf_op jit(solution)/shard_map/dot_general | solution.py:67
  (4 shorter events, 0.0 us)
Async XLA Ops:
  9.8 14.2 %copy-start.4 = (s32[8]{0:T(128)S(1)}, s32[8]{0:T(128)}, u32[]{:S(2)}) copy-start(s32[8]{0:T(128)} %param.9) | copy-start | bytes 100
  9.8 14.3 %copy-start.5 = (s32[64]{0:T(128)S(1)}, s32[64]{0:T(128)}, u32[]{:S(2)}) copy-start(s32[64]{0:T(128)} %param.10) | copy-start | bytes 772
  9.8 109.4 %all-to-all-start = ((f32[64,128,128]{2,1,0:T(8,128)}), f32[64,128,128]{2,1,0:T(8,128)}, u32[]{:S(2)}, u32[]{:S(2)}) async-start(f32[64,128,128]{2,1,0:T(8,128)} %stack.10), calls=%async_computation | async-start | bytes 8388608 | tf_op jit(solution)/shard_map/all_to_all | solution.py:11
  23.3 54.4 %all-gather.2.cloned.1.call-start = ((), (), s32[]{:S(2)}) async-start(), calls=%async_computation.5 | async-start | bytes 5242880 | tf_op jit(solution)/shard_map/all_gather | solution.py:62
  129.5 6.1 %copy-start = (s32[7]{0:T(128)S(1)}, s32[7]{0:T(128)}, u32[]{:S(2)}) copy-start(s32[7]{0:T(128)} %param.8) | copy-start | bytes 88
  129.5 7.0 %copy-start.3 = (s32[7,64]{1,0:T(8,128)S(1)}, s32[7,64]{1,0:T(8,128)}, u32[]{:S(2)}) copy-start(s32[7,64]{1,0:T(8,128)} %param.11) | copy-start | bytes 5380
  129.5 102.0 %copy-start.2 = (f32[128,128]{1,0:T(8,128)S(1)}, f32[128,128]{1,0:T(8,128)}, u32[]{:S(2)}) copy-start(f32[128,128]{1,0:T(8,128)} %param.7) | copy-start | bytes 196612
  129.5 102.0 %all-to-all-start.1 = ((f32[64,128,128]{2,1,0:T(8,128)}), f32[64,128,128]{2,1,0:T(8,128)}, u32[]{:S(2)}, u32[]{:S(2)}) async-start(f32[64,128,128]{2,1,0:T(8,128)} %stack.11), calls=%async_computation.1 | async-start | bytes 8388608 | tf_op jit(solution)/shard_map/all_to_all | solution.py:11
  241.7 101.8 %all-to-all-start.2 = ((f32[64,128,128]{2,1,0:T(8,128)}), f32[64,128,128]{2,1,0:T(8,128)}, u32[]{:S(2)}, u32[]{:S(2)}) async-start(f32[64,128,128]{2,1,0:T(8,128)} %stack.12), calls=%async_computation.2 | async-start | bytes 8388608 | tf_op jit(solution)/shard_map/all_to_all | solution.py:11
  351.9 102.0 %copy-start.1 = (f32[128,8192]{1,0:T(8,128)S(1)}, f32[128,8192]{1,0:T(8,128)}, u32[]{:S(2)}) copy-start(f32[128,8192]{1,0:T(8,128)} %all-gather.2.cloned.1.call-done) | copy-start | bytes 12582916
  460.7 101.9 %all-to-all-start.4 = ((f32[64,128,128]{2,1,0:T(8,128)}), f32[64,128,128]{2,1,0:T(8,128)}, u32[]{:S(2)}, u32[]{:S(2)}) async-start(f32[64,128,128]{2,1,0:T(8,128)} %stack.14), calls=%async_computation.4 | async-start | bytes 8388608 | tf_op jit(solution)/shard_map/all_to_all | solution.py:11
Sparse Core Ops, SparseCore 0:
  26.0 51.7 all-gather.1
